TPU v7x, 512 devices: a whole 4x8x8 slice. The times are simulated.
512 devices in a mesh: boxes: 128 (over y, z, core), probe: 4 (over x).
Axes of the slice: x: 4, y: 8, z: 8, core: 2. Of those that a mesh axis runs over, the one named last changes fastest.
Arguments:
- probes: float32 [32, 1048576], P('probe', 'boxes'), may hold values from -0.3 to 0.3
- points: float32 [3, 1048576], P(None, 'boxes'), may hold values from -1 to 1, as said below
- near_list: int32 [4096, 6], P('boxes'), may hold values from -1 to 4095, as said below
- leaf_proxy: float32 [3, 262144], P(None, 'boxes'), may hold values from -1 to 1, as said below
- inner_proxy: float32 [3, 245760], P(None, 'boxes'), may hold values from -1 to 1, as said below
- top_proxy: float32 [3, 16128], replicated, may hold values from -1 to 1, as said below
- far_list: int32 [4096, 3], P('boxes'), may hold values from -1 to 4095, as said below
Outputs:
- kernel_product: float32 [32, 1048576], P('probe', 'boxes')
Inputs may be any that keep to these rules, and one draw needn't show every extreme that they name: `points`: points on the unit sphere, box by box along a curve over it. `leaf_proxy`: proxy points on the unit sphere. `inner_proxy`: proxy points on the unit sphere. `top_proxy`: proxy points on the unit sphere. `near_list`: row b holds b - 1, b, b + 1 (modulo 4096) and those of the three candidates of row b of far_list that are -1 there, in some order, live entries first, then -1; some row is full. `far_list`: in row b, slot 0 holds b - 2, slot 1 holds b + 2, slot 2 holds b + 3 for even b and b - 3 for odd b (all modulo 4096), or -1.
All inputs are finite; a program needn't handle non-finite values.
Results may differ from a plain program's by a relative error of at most 0.00013.
Values sent between devices are 32-bit elements; how exact they have to be, the bound alone decides.
A program may use at most 64 MiB of HBM per device.

v0:
```python
import jax
import jax.numpy as jnp
from jax import lax
from jax.sharding import PartitionSpec as P

BOXES_DEV = 32
P_SIZE = 256
R = 64
W = 3
INNER_DEV = 30
SHARPNESS = 0.05
NUGGET = 1.0
PRECISE = lax.Precision.HIGHEST


def with_halo(array, sides, width):
    for axis, dim in sides:
        size, length = (lax.axis_size(axis), array.shape[dim])
        up = [(i, (i + 1) % size) for i in range(size)]
        down = [(j, i) for i, j in up]
        last = lax.slice_in_dim(array, length - width, length, axis=dim)
        initial = lax.slice_in_dim(array, 0, width, axis=dim)
        before = lax.ppermute(last, axis, up)
        after = lax.ppermute(initial, axis, down)
        array = jnp.concatenate([before, array, after], axis=dim)
    return array


def kernel_matrix(left_points, right_points, kernel_scale):
    distance_sq = (left_points[0][..., :, None] - right_points[0][..., None, :]) ** 2
    distance_sq = distance_sq + (left_points[1][..., :, None] - right_points[1][..., None, :]) ** 2
    distance_sq = distance_sq + (left_points[2][..., :, None] - right_points[2][..., None, :]) ** 2
    return 1.0 / (1.0 + kernel_scale * distance_sq)


def interpolation(left_points, right_points, kernel_scale):
    values = kernel_matrix(left_points, right_points, kernel_scale)
    return values / jnp.sum(values, axis=-1, keepdims=True)


def body(probes, points, near_list, leaf_proxy, inner_proxy, top_proxy, far_list):
    groups = lax.axis_size("boxes")
    device = lax.axis_index("boxes")
    boxes_all = BOXES_DEV * groups
    kernel_scale = SHARPNESS * boxes_all
    rows_here = probes.shape[0]
    local_depth = BOXES_DEV.bit_length() - 1
    tree_depth = groups.bit_length() - 1
    live_slot = near_list >= 0
    slot_weight = live_slot.astype(jnp.float32)
    where_in = jnp.where(live_slot, (near_list - device * BOXES_DEV + W + boxes_all) % boxes_all, 0)
    box_points = points.reshape(3, BOXES_DEV, P_SIZE)
    stacked = jnp.concatenate([probes, points], axis=0)
    extended = with_halo(stacked, (("boxes", 1),), W * P_SIZE)
    extended = extended.reshape(rows_here + 3, BOXES_DEV + 2 * W, P_SIZE)

    def near_box(near_inputs):
        slot_index, slot_mask, targets = near_inputs
        near_tiles = jnp.take(extended, slot_index, axis=1)
        near_values = near_tiles[:rows_here] * slot_mask[None, :, None]
        kernel_block = kernel_matrix(near_tiles[rows_here:], targets[:, None, :], kernel_scale)
        return jnp.einsum("qns,nst->qt", near_values, kernel_block, precision=PRECISE)

    near_field = lax.map(near_box, (where_in, slot_weight, jnp.moveaxis(box_points, 1, 0)))
    near_field = jnp.moveaxis(near_field, 0, 1).reshape(rows_here, BOXES_DEV * P_SIZE)
    probe_tiles = probes.reshape(rows_here, BOXES_DEV, P_SIZE)
    leaf_points = leaf_proxy.reshape(3, BOXES_DEV, R)
    leaf_basis = interpolation(box_points, leaf_points, kernel_scale)
    inner_points = inner_proxy.reshape(3, INNER_DEV, R)
    top_points = top_proxy.reshape(3, top_proxy.shape[1] // R, R)

    def node_proxy(height, node_index):
        offset = 2 * groups - 2 * (groups >> height)
        return lax.dynamic_slice_in_dim(top_points, offset + node_index, 1, 1)

    proxies = [leaf_points]
    for height in range(1, local_depth):
        offset = BOXES_DEV - (BOXES_DEV >> height - 1)
        number = BOXES_DEV >> height
        proxies.append(inner_points[:, offset : offset + number, :])
    proxies.append(node_proxy(0, device))
    level_moments = [jnp.einsum("qbp,bpr->qbr", probe_tiles, leaf_basis, precision=PRECISE)]
    transfer_maps = []
    for height in range(local_depth):
        interp_map = interpolation(
            proxies[height], jnp.repeat(proxies[height + 1], 2, axis=1), kernel_scale
        )
        transfer_maps.append(interp_map)
        lifted = jnp.einsum("qnr,nrs->qns", level_moments[-1], interp_map, precision=PRECISE)
        level_moments.append(lifted.reshape(rows_here, -1, 2, R).sum(axis=2))
    pyramid = jnp.concatenate(
        [
            jnp.concatenate(level_moments[:local_depth], axis=1),
            jnp.concatenate([leaf_points, inner_points], axis=1),
        ],
        axis=0,
    )
    pyramid_nodes = pyramid.shape[1]
    spread = with_halo(pyramid, (("boxes", 1),), pyramid_nodes)
    local_couplings = []
    for height in range(local_depth):
        count = BOXES_DEV >> height
        start = 0 if height == 0 else 2 * BOXES_DEV - (BOXES_DEV >> height - 1)
        view = jnp.concatenate(
            [
                spread[:, block * pyramid_nodes + start : block * pyramid_nodes + start + count, :]
                for block in range(3)
            ],
            axis=1,
        )
        if height == 0:
            live_far = far_list >= 0
            slot_ids = [
                jnp.where(
                    live_far[:, slot],
                    (far_list[:, slot] - device * BOXES_DEV + BOXES_DEV + boxes_all) % boxes_all,
                    0,
                )
                for slot in range(3)
            ]
            slot_masks = [live_far[:, slot].astype(jnp.float32)[None, :, None] for slot in range(3)]
        else:
            node = jnp.arange(count, dtype=jnp.int32)
            third = jnp.where(node % 2 == 0, node + 3, node - 3)
            slot_ids = [node - 2 + count, node + 2 + count, third + count]
            slot_masks = [None, None, None]
        coupling = jnp.zeros((rows_here, count, R), jnp.float32)
        for slot in range(3):
            picked = jnp.take(view, slot_ids[slot], axis=1)
            kernel_block = kernel_matrix(picked[rows_here:], proxies[height], kernel_scale)
            source_moment = picked[:rows_here]
            if slot_masks[slot] is not None:
                source_moment = source_moment * slot_masks[slot]
            coupling = coupling + jnp.einsum(
                "qnr,nrs->qns", source_moment, kernel_block, precision=PRECISE
            )
        local_couplings.append(coupling)
    top_levels = tree_depth - 1
    level_points = []
    for height in range(top_levels):
        offset = 2 * groups - 2 * (groups >> height)
        level_points.append(top_points[:, offset : offset + (groups >> height), :])
    level_moments_top = [lax.all_gather(level_moments[local_depth], "boxes", axis=1, tiled=True)]
    edge_maps = []
    for height in range(top_levels - 1):
        interp_map = interpolation(
            level_points[height], jnp.repeat(level_points[height + 1], 2, axis=1), kernel_scale
        )
        edge_maps.append(interp_map)
        lifted = jnp.einsum("qnr,nrs->qns", level_moments_top[-1], interp_map, precision=PRECISE)
        level_moments_top.append(lifted.reshape(rows_here, -1, 2, R).sum(axis=2))
    top_couplings = []
    for height in range(top_levels):
        number = groups >> height
        node = device // 2**height
        third = jnp.where(node % 2 == 0, node + 3, node - 3) % number
        if number > 4:
            source_ids = [(node - 2) % number, (node + 2) % number, third]
        else:
            source_ids = [(node + 2) % number]
        target_points = lax.dynamic_slice_in_dim(level_points[height], node, 1, 1)
        coupling = jnp.zeros((rows_here, 1, R), jnp.float32)
        for source in source_ids:
            kernel_block = kernel_matrix(
                lax.dynamic_slice_in_dim(level_points[height], source, 1, 1),
                target_points,
                kernel_scale,
            )
            source_moment = lax.dynamic_slice_in_dim(level_moments_top[height], source, 1, 1)
            coupling = coupling + jnp.einsum(
                "qnr,nrs->qns", source_moment, kernel_block, precision=PRECISE
            )
        top_couplings.append(coupling)
    descent = top_couplings[-1]
    for height in range(top_levels - 2, -1, -1):
        own_edge = lax.dynamic_slice_in_dim(edge_maps[height], device // 2**height, 1, 0)
        descent = (
            jnp.einsum("qns,nrs->qnr", descent, own_edge, precision=PRECISE) + top_couplings[height]
        )
    for height in range(local_depth - 1, -1, -1):
        descent = jnp.einsum(
            "qns,nrs->qnr", jnp.repeat(descent, 2, axis=1), transfer_maps[height], precision=PRECISE
        )
        descent = descent + local_couplings[height]
    far_field = jnp.einsum("qbr,bpr->qbp", descent, leaf_basis, precision=PRECISE).reshape(
        rows_here, BOXES_DEV * P_SIZE
    )
    return near_field + far_field + NUGGET * probes


def solution(mesh):
    in_specs = (
        P("probe", "boxes"),
        P(None, "boxes"),
        P("boxes", None),
        P(None, "boxes"),
        P(None, "boxes"),
        P(),
        P("boxes", None),
    )
    out_specs = P("probe", "boxes")
    return jax.shard_map(body, mesh=mesh, in_specs=in_specs, out_specs=out_specs, check_vma=False)
```

profile of v0, /device:TPU:1, one launch (start us, length us, event | category | flops | bytes accessed | tf_op | source)
XLA Modules:
  0.0 403.7 jit_solution(18085279957621713053)
XLA Ops:
  3.1 1.3 slice_reduce_fusion.2
  5.6 3.8 constant_dynamic-update-slice_fusion.6
  9.6 1.4 divide_reduce_fusion.4
  11.0 2.6 bitcast_reduce_fusion.3
  14.4 1.3 bitcast_reduce_fusion.5
  18.6 8.8 %collective-permute-start.3 = (f32[11,62,64]{2,0,1:T(8,128)S(1)}, f32[11,62,64]{2,0,1:T(8,128)}, u32[]{:S(2)}, u32[]{:S(2)}) collective-permute-start(f32[11,62,64]{2,0,1:T(8,128)S(1)} %maximum_maximum_fusion), channel_id=1, source_target_pairs={{4,0},{8,4},{12,8},{16,12},{20,16},{24,20},{28,24},{32,28},{36,32}... | collective-permute-start | bytes 523784 | tf_op jit(solution)/shard_map/ppermute | solution.py:24
  27.4 1.9 collective-permute-start.2
  30.1 1.9 collective-permute-start
  32.0 7.9 %collective-permute-start.1 = (f32[11,768]{1,0:T(8,128)}, f32[11,768]{1,0:T(8,128)}, u32[]{:S(2)}, u32[]{:S(2)}) collective-permute-start(f32[11,768]{1,0:T(8,128)} %get-tuple-element.106), channel_id=1, source_target_pairs={{4,0},{8,4},{12,8},{16,12},{20,16},{24,20},{28,24},{32,28},{36,32}... | collective-permute-start | bytes 101384 | tf_op jit(solution)/shard_map/ppermute | solution.py:24
  58.8 52.1 %all-gather.1 = f32[128,64,8]{1,2,0:T(8,128)S(1)} all-gather(f32[1,64,8]{1,2,0:T(8,128)S(1)} %convolution_bitcast_fusion.3), channel_id=2, replica_groups=mesh['boxes'=128,'probe'=4] {'boxes'}, dimensions={0}, use_global_device_ids=true | all-gather | bytes 264192 | tf_op jit(solution)/shard_map/all_gather | solution.py:143
  111.5 5.6 %divide_reduce_fusion = f32[128,64]{1,0:T(8,128)S(1)} fusion(f32[128,64]{1,0:T(8,128)S(1)} %bitcast.618, f32[128,64]{1,0:T(8,128)S(1)} %get-tuple-element.123, f32[128,64]{1,0:T(8,128)S(1)} %bitcast.621, f32[128,64]{1,0:T(8,128)S(1)} %get-tuple-element.124, f32[128,64]{1,0:T(8,128)S(1)} %bitcast.615, f32[128,64]{1,0:T(8,128)S(1)} %get-tuple-element.122), kind=kLoop, calls=%fused_computation.49 | loop fusion | flops 6283264 | bytes 229376 | tf_op jit(solution)/shard_map/reduce_sum | solution.py:38
  117.1 6.3 %multiply_divide_fusion = f32[128,64,64]{2,1,0:T(8,128)} fusion(f32[128,64]{1,0:T(8,128)S(1)} %divide_reduce_fusion, f32[128,64]{1,0:T(8,128)S(1)} %bitcast.619, f32[128,64]{1,0:T(8,128)S(1)} %get-tuple-element.123, f32[128,64]{1,0:T(8,128)S(1)} %bitcast.622, f32[128,64]{1,0:T(8,128)S(1)} %get-tuple-element.124, f32[128,64]{1,0:T(8,128)S(1)} %bitcast.616, ...), kind=kLoop, calls=%fused_computation.47 | loop fusion | flops 6291456 | bytes 2326528 | tf_op jit(solution)/shard_map/div | solution.py:38
  123.4 10.2 %bitcast_reduce_fusion = f32[8,64,64]{2,0,1:T(8,128)S(1)} fusion(f32[8,128,64]{2,1,0:T(8,128)S(1)} %reshape.5058, f32[128,64]{1,0:T(8,128)S(1)} %divide_reduce_fusion, f32[128,64]{1,0:T(8,128)S(1)} %bitcast.620, f32[128,64]{1,0:T(8,128)S(1)} %get-tuple-element.123, f32[128,64]{1,0:T(8,128)S(1)} %bitcast.623, f32[128,64]{1,0:T(8,128)S(1)} %get-tuple-element.124, ...), kind=kOutput, calls=%fused_computation.131 | convolution fusion | flops 56655872 | bytes 622592 | tf_op jit(solution)/shard_map/qnr,nrs->qns/dot_general | solution.py:150
  133.8 2.7 divide_reduce_fusion.1
  136.5 3.1 multiply_divide_fusion.1
  139.7 5.1 %bitcast_reduce_fusion.1 = f32[8,32,64]{2,0,1:T(8,128)S(1)} fusion(f32[8,64,64]{2,0,1:T(8,128)S(1)} %bitcast_reduce_fusion, f32[64,64]{1,0:T(8,128)S(1)} %divide_reduce_fusion.1, f32[64,64]{1,0:T(8,128)S(1)} %bitcast.630, f32[64,64]{1,0:T(8,128)S(1)} %copy-done.5, f32[64,64]{1,0:T(8,128)S(1)} %bitcast.633, f32[64,64]{1,0:T(8,128)S(1)} %copy-done.7, ...), kind=kOutput, calls=%fused_computation.189 | convolution fusion | flops 28327936 | bytes 311296 | tf_op jit(solution)/shard_map/qnr,nrs->qns/dot_general | solution.py:150
  144.9 1.4 divide_reduce_fusion.3
  146.3 2.1 multiply_divide_fusion.3
  148.4 2.6 bitcast_reduce_fusion.2
  151.7 1.4 multiply_divide_fusion.7
  153.1 1.3 bitcast_reduce_fusion.4
  155.1 1.2 bitcast_reduce_fusion.6
  176.6 182.3 %while.10 = (s32[]{:T(128)}, f32[32,8,256]{2,1,0:T(8,128)}, s32[32,6]{1,0:T(8,128)}, f32[11,38,256]{2,0,1:T(8,128)S(1)}, f32[32,6]{1,0:T(8,128)}, /*index=5*/f32...) while((s32[]{:T(128)}, f32[32,8,256]{2,1,0:T(8,128)}, s32[32,6]{1,0:T(8,128)}, ...), condition=%wide.region_1.2_spmd, body=%wide.region_0.1_spmd.sunk | while | flops 42104376 | bytes 440149 | solution.py:64
  180.2 2.2 fusion.862
  185.8 2.2 fusion.862
  191.5 2.2 fusion.862
  197.2 2.2 fusion.862
  202.8 2.2 fusion.862
  208.5 2.2 fusion.862
  214.2 2.2 fusion.862
  219.8 2.2 fusion.862
  225.5 2.2 fusion.862
  231.3 2.2 fusion.862
  237.0 2.2 fusion.862
  242.7 2.2 fusion.862
  248.4 2.2 fusion.862
  254.1 2.2 fusion.862
  259.8 2.2 fusion.862
  265.5 2.2 fusion.862
  271.2 2.2 fusion.862
  276.9 2.2 fusion.862
  282.6 2.2 fusion.862
  288.3 2.2 fusion.862
  294.0 2.2 fusion.862
  299.7 2.2 fusion.862
  305.4 2.2 fusion.862
  311.1 2.2 fusion.862
  316.8 2.2 fusion.862
  322.5 2.2 fusion.862
  328.2 2.2 fusion.862
  333.9 2.2 fusion.862
  339.6 2.2 fusion.862
  345.3 2.2 fusion.862
  351.0 2.2 fusion.862
  356.7 2.2 fusion.862
  384.5 1.6 fusion.145
  386.1 1.2 fusion.102
  387.3 1.2 convolution_add_fusion.4
  388.6 2.3 fusion.54
  390.9 2.3 convolution_add_fusion.1
  393.3 2.3 convolution_add_fusion
  395.6 1.2 fusion.19
  396.9 3.2 fusion.17
  400.2 2.7 fusion.16
  (824 shorter events, 186.3 us)
Async XLA Ops:
  0.9 56.1 %copy-start.82 = (f32[2,64]{1,0:T(2,128)}, f32[2,64]{1,0:T(2,128)S(1)}, u32[]{:S(2)}) copy-start(f32[2,64]{1,0:T(2,128)S(1)} %get-tuple-element.194) | copy-start | bytes 1540
  0.9 56.1 %copy-start.84 = (f32[2,64]{1,0:T(2,128)}, f32[2,64]{1,0:T(2,128)S(1)}, u32[]{:S(2)}) copy-start(f32[2,64]{1,0:T(2,128)S(1)} %get-tuple-element.195) | copy-start | bytes 1540
  0.9 56.1 %copy-start.86 = (f32[2,64]{1,0:T(2,128)}, f32[2,64]{1,0:T(2,128)S(1)}, u32[]{:S(2)}) copy-start(f32[2,64]{1,0:T(2,128)S(1)} %get-tuple-element.196) | copy-start | bytes 1540
  0.9 17.1 %copy-start.66 = (f32[4,64]{1,0:T(4,128)}, f32[4,64]{1,0:T(4,128)S(1)}, u32[]{:S(2)}) copy-start(f32[4,64]{1,0:T(4,128)S(1)} %get-tuple-element.197) | copy-start | bytes 3076
  0.9 17.0 %copy-start.68 = (f32[4,64]{1,0:T(4,128)}, f32[4,64]{1,0:T(4,128)S(1)}, u32[]{:S(2)}) copy-start(f32[4,64]{1,0:T(4,128)S(1)} %get-tuple-element.198) | copy-start | bytes 3076
  0.9 17.0 %copy-start.70 = (f32[4,64]{1,0:T(4,128)}, f32[4,64]{1,0:T(4,128)S(1)}, u32[]{:S(2)}) copy-start(f32[4,64]{1,0:T(4,128)S(1)} %get-tuple-element.199) | copy-start | bytes 3076
  0.9 15.2 %copy-start.52 = (f32[8,64]{1,0:T(8,128)}, f32[8,64]{1,0:T(8,128)S(1)}, u32[]{:S(2)}) copy-start(f32[8,64]{1,0:T(8,128)S(1)} %get-tuple-element.200) | copy-start | bytes 6148
  0.9 15.2 %copy-start.54 = (f32[8,64]{1,0:T(8,128)}, f32[8,64]{1,0:T(8,128)S(1)}, u32[]{:S(2)}) copy-start(f32[8,64]{1,0:T(8,128)S(1)} %get-tuple-element.201) | copy-start | bytes 6148
  1.0 15.2 %copy-start.56 = (f32[8,64]{1,0:T(8,128)}, f32[8,64]{1,0:T(8,128)S(1)}, u32[]{:S(2)}) copy-start(f32[8,64]{1,0:T(8,128)S(1)} %get-tuple-element.202) | copy-start | bytes 6148
  1.0 13.4 %copy-start.30 = (f32[16,64]{1,0:T(8,128)}, f32[16,64]{1,0:T(8,128)S(1)}, u32[]{:S(2)}) copy-start(f32[16,64]{1,0:T(8,128)S(1)} %get-tuple-element.203) | copy-start | bytes 12292
  1.0 13.4 %copy-start.32 = (f32[16,64]{1,0:T(8,128)}, f32[16,64]{1,0:T(8,128)S(1)}, u32[]{:S(2)}) copy-start(f32[16,64]{1,0:T(8,128)S(1)} %get-tuple-element.204) | copy-start | bytes 12292
  1.0 13.4 %copy-start.34 = (f32[16,64]{1,0:T(8,128)}, f32[16,64]{1,0:T(8,128)S(1)}, u32[]{:S(2)}) copy-start(f32[16,64]{1,0:T(8,128)S(1)} %get-tuple-element.205) | copy-start | bytes 12292
  2.9 8.0 %copy-start.16 = (f32[32,64]{1,0:T(8,128)}, f32[32,64]{1,0:T(8,128)S(1)}, u32[]{:S(2)}) copy-start(f32[32,64]{1,0:T(8,128)S(1)} %sub.2636) | copy-start | bytes 24580
  3.0 8.0 %copy-start.18 = (f32[32,64]{1,0:T(8,128)}, f32[32,64]{1,0:T(8,128)S(1)}, u32[]{:S(2)}) copy-start(f32[32,64]{1,0:T(8,128)S(1)} %sub.2641) | copy-start | bytes 24580
  3.1 7.9 %copy-start.20 = (f32[32,64]{1,0:T(8,128)}, f32[32,64]{1,0:T(8,128)S(1)}, u32[]{:S(2)}) copy-start(f32[32,64]{1,0:T(8,128)S(1)} %sub.2646) | copy-start | bytes 24580
  15.7 13.7 %copy-start.1 = (f32[8,8192]{1,0:T(8,128)S(1)}, f32[8,8192]{1,0:T(8,128)}, u32[]{:S(2)}) copy-start(f32[8,8192]{1,0:T(8,128)} %param.19) | copy-start | bytes 786436
  15.7 13.7 %copy-start.8 = (f32[3,8192]{1,0:T(4,128)S(1)}, f32[3,8192]{1,0:T(4,128)}, u32[]{:S(2)}) copy-start(f32[3,8192]{1,0:T(4,128)} %param.20) | copy-start | bytes 294916
  17.6 28.4 %copy-start.96 = (s32[32,3]{0,1:T(4,128)S(1)}, s32[32,3]{0,1:T(4,128)}, u32[]{:S(2)}) copy-start(s32[32,3]{0,1:T(4,128)} %param.25) | copy-start | bytes 1156
  17.6 29.7 %copy-start.97 = (s32[32,6]{0,1:T(8,128)S(1)}, s32[32,6]{0,1:T(8,128)}, u32[]{:S(2)}) copy-start(s32[32,6]{0,1:T(8,128)} %param.21) | copy-start | bytes 2308
  17.6 31.0 %copy-start.15 = (f32[3,16128]{1,0:T(4,128)S(1)}, f32[3,16128]{1,0:T(4,128)}, u32[]{:S(2)}) copy-start(f32[3,16128]{1,0:T(4,128)} %param.24) | copy-start | bytes 580612
  17.6 30.3 %copy-start.90 = (f32[2,2,64]{2,1,0:T(2,128)}, f32[2,2,64]{2,1,0:T(2,128)S(1)}, u32[]{:S(2)}) copy-start(f32[2,2,64]{2,1,0:T(2,128)S(1)} %broadcast_in_dim.234) | copy-start | bytes 3076
  17.7 30.3 %copy-start.92 = (f32[2,2,64]{2,1,0:T(2,128)}, f32[2,2,64]{2,1,0:T(2,128)S(1)}, u32[]{:S(2)}) copy-start(f32[2,2,64]{2,1,0:T(2,128)S(1)} %broadcast_in_dim.238) | copy-start | bytes 3076
  17.7 30.3 %copy-start.94 = (f32[2,2,64]{2,1,0:T(2,128)}, f32[2,2,64]{2,1,0:T(2,128)S(1)}, u32[]{:S(2)}) copy-start(f32[2,2,64]{2,1,0:T(2,128)S(1)} %broadcast_in_dim.236) | copy-start | bytes 3076
  18.6 340.3 %collective-permute-start.3 = (f32[11,62,64]{2,0,1:T(8,128)S(1)}, f32[11,62,64]{2,0,1:T(8,128)}, u32[]{:S(2)}, u32[]{:S(2)}) collective-permute-start(f32[11,62,64]{2,0,1:T(8,128)S(1)} %maximum_maximum_fusion), channel_id=1, source_target_pairs={{4,0},{8,4},{12,8},{16,12},{20,16},{24,20},{28,24},{32,28},{36,32}... | collective-permute-start | bytes 523784 | tf_op jit(solution)/shard_map/ppermute | solution.py:24
  27.4 332.2 %collective-permute-start.2 = (f32[11,62,64]{2,0,1:T(8,128)S(1)}, f32[11,62,64]{2,0,1:T(8,128)}, u32[]{:S(2)}, u32[]{:S(2)}) collective-permute-start(f32[11,62,64]{2,0,1:T(8,128)S(1)} %maximum_maximum_fusion), channel_id=1, source_target_pairs={{0,4},{4,8},{8,12},{12,16},{16,20},{20,24},{24,28},{28,32},{32,36}... | collective-permute-start | bytes 523784 | tf_op jit(solution)/shard_map/ppermute | solution.py:23
  30.1 145.3 %collective-permute-start = (f32[11,768]{1,0:T(8,128)}, f32[11,768]{1,0:T(8,128)}, u32[]{:S(2)}, u32[]{:S(2)}) collective-permute-start(f32[11,768]{1,0:T(8,128)} %get-tuple-element.105), channel_id=1, source_target_pairs={{0,4},{4,8},{8,12},{12,16},{16,20},{20,24},{24,28},{28,32},{32,36}... | collective-permute-start | bytes 101384 | tf_op jit(solution)/shard_map/ppermute | solution.py:23
  32.0 143.4 %collective-permute-start.1 = (f32[11,768]{1,0:T(8,128)}, f32[11,768]{1,0:T(8,128)}, u32[]{:S(2)}, u32[]{:S(2)}) collective-permute-start(f32[11,768]{1,0:T(8,128)} %get-tuple-element.106), channel_id=1, source_target_pairs={{4,0},{8,4},{12,8},{16,12},{20,16},{24,20},{28,24},{32,28},{36,32}... | collective-permute-start | bytes 101384 | tf_op jit(solution)/shard_map/ppermute | solution.py:24
  48.8 62.4 %copy-start = (f32[3,252,64]{2,1,0:T(8,128)}, f32[3,252,64]{2,1,0:T(8,128)S(1)}, u32[]{:S(2)}) copy-start(f32[3,252,64]{2,1,0:T(8,128)S(1)} %reshape.4884) | copy-start | bytes 580612
  49.4 9.4 %copy-start.36 = (f32[8,64]{1,0:T(8,128)}, f32[8,64]{1,0:T(8,128)S(1)}, u32[]{:S(2)}) copy-start(f32[8,64]{1,0:T(8,128)S(1)} %get-tuple-element.114) | copy-start | bytes 6148
  49.4 9.4 %copy-start.38 = (f32[8,64]{1,0:T(8,128)}, f32[8,64]{1,0:T(8,128)S(1)}, u32[]{:S(2)}) copy-start(f32[8,64]{1,0:T(8,128)S(1)} %get-tuple-element.115) | copy-start | bytes 6148
  50.1 83.6 %copy-start.9 = (f32[32,64]{1,0:T(8,128)}, f32[32,64]{1,0:T(8,128)S(1)}, u32[]{:S(2)}) copy-start(f32[32,64]{1,0:T(8,128)S(1)} %get-tuple-element.119) | copy-start | bytes 24580
  50.1 83.6 %copy-start.11 = (f32[32,64]{1,0:T(8,128)}, f32[32,64]{1,0:T(8,128)S(1)}, u32[]{:S(2)}) copy-start(f32[32,64]{1,0:T(8,128)S(1)} %get-tuple-element.120) | copy-start | bytes 24580
  50.1 83.7 %copy-start.13 = (f32[32,64]{1,0:T(8,128)}, f32[32,64]{1,0:T(8,128)S(1)}, u32[]{:S(2)}) copy-start(f32[32,64]{1,0:T(8,128)S(1)} %get-tuple-element.121) | copy-start | bytes 24580
  50.1 83.7 %copy-start.4 = (f32[64,64]{1,0:T(8,128)}, f32[64,64]{1,0:T(8,128)S(1)}, u32[]{:S(2)}) copy-start(f32[64,64]{1,0:T(8,128)S(1)} %get-tuple-element.126) | copy-start | bytes 49156
  50.1 83.7 %copy-start.6 = (f32[64,64]{1,0:T(8,128)}, f32[64,64]{1,0:T(8,128)S(1)}, u32[]{:S(2)}) copy-start(f32[64,64]{1,0:T(8,128)S(1)} %get-tuple-element.127) | copy-start | bytes 49156
  111.4 12.0 %copy-start.3 = (f32[8,128,64]{2,1,0:T(8,128)}, f32[8,128,64]{2,1,0:T(8,128)S(1)}, u32[]{:S(2)}) copy-start(f32[8,128,64]{2,1,0:T(8,128)S(1)} %reshape.5058) | copy-start | bytes 786436
  133.6 11.2 %copy-start.132 = (f32[8,64,64]{2,0,1:T(8,128)}, f32[8,64,64]{2,0,1:T(8,128)S(1)}, u32[]{:S(2)}) copy-start(f32[8,64,64]{2,0,1:T(8,128)S(1)} %bitcast_reduce_fusion) | copy-start | bytes 393220
  144.8 6.1 %copy-start.133 = (f32[8,32,64]{2,0,1:T(8,128)}, f32[8,32,64]{2,0,1:T(8,128)S(1)}, u32[]{:S(2)}) copy-start(f32[8,32,64]{2,0,1:T(8,128)S(1)} %bitcast_reduce_fusion.1) | copy-start | bytes 196612
  153.1 6.7 %slice-start = ((f32[3,252,64]{2,1,0:T(8,128)}), f32[3,8,64]{2,1,0:T(8,128)S(1)}, s32[]{:S(2)}) async-start(f32[3,252,64]{2,1,0:T(8,128)} %copy-done), calls=%async_computation | async-start | bytes 24576 | tf_op jit(solution)/shard_map/slice | solution.py:142
  153.1 6.7 %slice-start.2 = ((f32[3,252,64]{2,1,0:T(8,128)}), f32[3,32,64]{2,1,0:T(8,128)S(1)}, s32[]{:S(2)}) async-start(f32[3,252,64]{2,1,0:T(8,128)} %copy-done), calls=%async_computation.2 | async-start | bytes 98304 | tf_op jit(solution)/shard_map/slice | solution.py:142
  155.0 8.6 %slice-start.1 = ((f32[3,252,64]{2,1,0:T(8,128)}), f32[3,16,64]{2,1,0:T(8,128)S(1)}, s32[]{:S(2)}) async-start(f32[3,252,64]{2,1,0:T(8,128)} %copy-done), calls=%async_computation.1 | async-start | bytes 49152 | tf_op jit(solution)/shard_map/slice | solution.py:142
  155.0 8.6 %slice-start.3 = ((f32[3,252,64]{2,1,0:T(8,128)}), f32[3,64,64]{2,1,0:T(8,128)S(1)}, s32[]{:S(2)}) async-start(f32[3,252,64]{2,1,0:T(8,128)} %copy-done), calls=%async_computation.3 | async-start | bytes 196608 | tf_op jit(solution)/shard_map/slice | solution.py:142
  156.3 18.5 %copy-start.83 = (f32[2,64]{1,0:T(2,128)S(1)}, f32[2,64]{1,0:T(2,128)}, u32[]{:S(2)}) copy-start(f32[2,64]{1,0:T(2,128)} %copy-done.82) | copy-start | bytes 1540
  156.3 18.5 %copy-start.85 = (f32[2,64]{1,0:T(2,128)S(1)}, f32[2,64]{1,0:T(2,128)}, u32[]{:S(2)}) copy-start(f32[2,64]{1,0:T(2,128)} %copy-done.84) | copy-start | bytes 1540
  156.3 18.6 %copy-start.87 = (f32[2,64]{1,0:T(2,128)S(1)}, f32[2,64]{1,0:T(2,128)}, u32[]{:S(2)}) copy-start(f32[2,64]{1,0:T(2,128)} %copy-done.86) | copy-start | bytes 1540
  156.3 18.6 %copy-start.107 = (f32[64]{0:T(128)S(1)}, f32[64]{0:T(128)}, u32[]{:S(2)}) copy-start(f32[64]{0:T(128)} %copy-done.106) | copy-start | bytes 772
  156.3 18.6 %copy-start.109 = (f32[64]{0:T(128)S(1)}, f32[64]{0:T(128)}, u32[]{:S(2)}) copy-start(f32[64]{0:T(128)} %copy-done.108) | copy-start | bytes 772
  156.3 18.6 %copy-start.111 = (f32[64]{0:T(128)S(1)}, f32[64]{0:T(128)}, u32[]{:S(2)}) copy-start(f32[64]{0:T(128)} %copy-done.110) | copy-start | bytes 772
  156.3 18.6 %copy-start.113 = (f32[2,64]{1,0:T(2,128)S(1)}, f32[2,64]{1,0:T(2,128)}, u32[]{:S(2)}) copy-start(f32[2,64]{1,0:T(2,128)} %copy-done.112) | copy-start | bytes 1540
  159.9 15.3 %copy-start.126 = (s32[4]{0:T(128)S(1)}, s32[4]{0:T(128)}, u32[]{:S(2)}) copy-start(s32[4]{0:T(128)} %compare_select_fusion.13) | copy-start | bytes 52
  159.9 15.3 %copy-start.127 = (s32[8]{0:T(128)S(1)}, s32[8]{0:T(128)}, u32[]{:S(2)}) copy-start(s32[8]{0:T(128)} %compare_select_fusion.10) | copy-start | bytes 100
  159.9 15.3 %copy-start.105 = (s32[32]{0:T(128)S(1)}, s32[32]{0:T(128)}, u32[]{:S(2)}) copy-start(s32[32]{0:T(128)} %get-tuple-element.257) | copy-start | bytes 388
  159.9 15.3 %copy-start.125 = (s32[16]{0:T(128)S(1)}, s32[16]{0:T(128)}, u32[]{:S(2)}) copy-start(s32[16]{0:T(128)} %compare_select_fusion.7) | copy-start | bytes 196
  176.6 184.5 %copy-start.124 = (pred[2]{0:T(512)(128)(4,1)S(1)}, pred[2]{0:T(512)(128)(4,1)}, u32[]{:S(2)}) copy-start(pred[2]{0:T(512)(128)(4,1)} %get-tuple-element.277) | copy-start | bytes 10
  176.6 185.9 %copy-start.123 = (pred[2]{0:T(512)(128)(4,1)S(1)}, pred[2]{0:T(512)(128)(4,1)}, u32[]{:S(2)}) copy-start(pred[2]{0:T(512)(128)(4,1)} %get-tuple-element.278) | copy-start | bytes 10
  176.6 186.0 %copy-start.122 = (pred[2]{0:T(512)(128)(4,1)S(1)}, pred[2]{0:T(512)(128)(4,1)}, u32[]{:S(2)}) copy-start(pred[2]{0:T(512)(128)(4,1)} %broadcast_compare_fusion.2) | copy-start | bytes 10
  176.6 188.3 %copy-start.121 = (pred[4]{0:T(512)(128)(4,1)S(1)}, pred[4]{0:T(512)(128)(4,1)}, u32[]{:S(2)}) copy-start(pred[4]{0:T(512)(128)(4,1)} %get-tuple-element.275) | copy-start | bytes 16
  176.6 189.6 %copy-start.120 = (pred[4]{0:T(512)(128)(4,1)S(1)}, pred[4]{0:T(512)(128)(4,1)}, u32[]{:S(2)}) copy-start(pred[4]{0:T(512)(128)(4,1)} %get-tuple-element.276) | copy-start | bytes 16
  176.6 189.7 %copy-start.119 = (pred[4]{0:T(512)(128)(4,1)S(1)}, pred[4]{0:T(512)(128)(4,1)}, u32[]{:S(2)}) copy-start(pred[4]{0:T(512)(128)(4,1)} %compare_and_fusion.12) | copy-start | bytes 16
  176.6 192.2 %copy-start.118 = (pred[8]{0:T(512)(128)(4,1)S(1)}, pred[8]{0:T(512)(128)(4,1)}, u32[]{:S(2)}) copy-start(pred[8]{0:T(512)(128)(4,1)} %get-tuple-element.273) | copy-start | bytes 28
  358.9 11.3 %copy-start.117 = (pred[8]{0:T(512)(128)(4,1)S(1)}, pred[8]{0:T(512)(128)(4,1)}, u32[]{:S(2)}) copy-start(pred[8]{0:T(512)(128)(4,1)} %get-tuple-element.274) | copy-start | bytes 28
  358.9 11.4 %copy-start.116 = (pred[8]{0:T(512)(128)(4,1)S(1)}, pred[8]{0:T(512)(128)(4,1)}, u32[]{:S(2)}) copy-start(pred[8]{0:T(512)(128)(4,1)} %compare_and_fusion.9) | copy-start | bytes 28
  358.9 14.0 %copy-start.115 = (pred[16]{0:T(512)(128)(4,1)S(1)}, pred[16]{0:T(512)(128)(4,1)}, u32[]{:S(2)}) copy-start(pred[16]{0:T(512)(128)(4,1)} %get-tuple-element.271) | copy-start | bytes 52
  363.4 10.9 %copy-start.114 = (pred[16]{0:T(512)(128)(4,1)S(1)}, pred[16]{0:T(512)(128)(4,1)}, u32[]{:S(2)}) copy-start(pred[16]{0:T(512)(128)(4,1)} %get-tuple-element.272) | copy-start | bytes 52
  (81 other events, 219.1 us)
where the time goes:
time: 410 us; the launch traced here: 404 us
  matrix products  138 us (34%)
  local copies, waits for them, and re-layouts  95.9 us (23%)
  other arithmetic  92.4 us (23%)
  blocking collectives  52.1 us (13%)
  starting transfers between devices  20.5 us (5%)
    dot_general x32, matrix products, near_box(): jnp.einsum('qns,nst->qt', near_values, kernel_block, precision=PRECISE)  68.9 us
    all_gather x1, blocking collectives, body(): lax.all_gather(level_moments[local_depth], 'boxes', axis=1, tiled=True)  52.1 us
    slice x42, local copies, waits for them, and re-layouts, kernel_matrix(): right_points[0][..., None, :]  27.3 us
    dot_general x31, matrix products, body(): jnp.einsum('qnr,nrs->qns', source_moment, kernel_block, precision=PRECISE)  26.9 us
    select_n x64, other arithmetic, near_box(): near_tiles = jnp.take(extended, slot_index, axis=1)  24.3 us
    and x32, other arithmetic, near_box(): near_tiles = jnp.take(extended, slot_index, axis=1)  21.9 us
    mul x32, local copies, waits for them, and re-layouts, near_box(): near_values = near_tiles[:rows_here] * slot_mask[None, :, None]  21.8 us
    dot_general x5, matrix products, body(): jnp.einsum('qnr,nrs->qns', level_moments_top[-1], interp_map, precision=P...  20.4 us
  transfers between devices with their start and end apart: 4, of which 0 were waited for; matrix products, arithmetic and copies ran while one was open for 66% of the time, Pallas kernels for 0%

commit v1 on v0

--- a/solution.py
+++ b/solution.py
@@ -1,7 +1,9 @@
+import functools
 import jax
 import jax.numpy as jnp
 from jax import lax
 from jax.sharding import PartitionSpec as P
+from jax.lax import all_to_all, psum
 
 BOXES_DEV = 32
 P_SIZE = 256
@@ -11,6 +13,16 @@
 SHARPNESS = 0.05
 NUGGET = 1.0
 PRECISE = lax.Precision.HIGHEST
+
+
+def pack_vectors(panel, axis_name):
+    spare = jnp.concatenate(
+        all_to_all(jnp.stack([panel for _ in range(psum(1, axis_name))]), axis_name, 0, 0), axis=1
+    )
+    return spare
+
+
+unite_quotas_here = functools.partial(pack_vectors, axis_name="boxes")
 
 
 def with_halo(array, sides, width):
@@ -140,7 +152,7 @@
     for height in range(top_levels):
         offset = 2 * groups - 2 * (groups >> height)
         level_points.append(top_points[:, offset : offset + (groups >> height), :])
-    level_moments_top = [lax.all_gather(level_moments[local_depth], "boxes", axis=1, tiled=True)]
+    level_moments_top = [unite_quotas_here(level_moments[local_depth])]
     edge_maps = []
     for height in range(top_levels - 1):
         interp_map = interpolation(

time: 410 us -> 472 us (1.15)
  the two profiles are of different devices: /device:TPU:1 before, /device:TPU:6 now
where the time goes in v1:
time: 472 us; the launch traced here: 465 us
  matrix products  165 us (35%)
  local copies, waits for them, and re-layouts  153 us (32%)
  other arithmetic  106 us (22%)
  starting transfers between devices  34.5 us (7%)
  between operations  4.88 us (1%)
    dot_general x32, matrix products, near_box(): jnp.einsum('qns,nst->qt', near_values, kernel_block, precision=PRECISE)  90.9 us
    slice x42, local copies, waits for them, and re-layouts, kernel_matrix(): right_points[0][..., None, :]  45.5 us
    mul x32, local copies, waits for them, and re-layouts, near_box(): near_values = near_tiles[:rows_here] * slot_mask[None, :, None]  40.1 us
    dot_general x31, matrix products, body(): jnp.einsum('qnr,nrs->qns', source_moment, kernel_block, precision=PRECISE)  31.7 us
    select_n x64, other arithmetic, near_box(): near_tiles = jnp.take(extended, slot_index, axis=1)  24.4 us
    and x32, other arithmetic, near_box(): near_tiles = jnp.take(extended, slot_index, axis=1)  22 us
    dot_general x5, matrix products, body(): jnp.einsum('qnr,nrs->qns', level_moments_top[-1], interp_map, precision=P...  20.7 us
    ppermute x2, starting transfers between devices, with_halo(): after = lax.ppermute(initial, axis, down)  20.4 us
  transfers between devices with their start and end apart: 5, of which 0 were waited for; matrix products, arithmetic and copies ran while one was open for 75% of the time, Pallas kernels for 0%

profile of v1, /device:TPU:6, one launch (start us, length us, event | category | flops | bytes accessed | tf_op | source)
XLA Modules:
  0.0 465.4 jit_solution(11694956248658193939)
XLA Ops:
  5.6 3.8 constant_dynamic-update-slice_fusion.6
  11.0 2.6 bitcast_reduce_fusion.3
  17.7 13.4 %collective-permute-start.3 = (f32[11,62,64]{2,0,1:T(8,128)S(1)}, f32[11,62,64]{2,0,1:T(8,128)}, u32[]{:S(2)}, u32[]{:S(2)}) collective-permute-start(f32[11,62,64]{2,0,1:T(8,128)S(1)} %maximum_maximum_fusion), channel_id=1, source_target_pairs={{4,0},{8,4},{12,8},{16,12},{20,16},{24,20},{28,24},{32,28},{36,32}... | collective-permute-start | bytes 523784 | tf_op jit(solution)/shard_map/ppermute | solution.py:36
  31.2 1.9 collective-permute-start.2
  36.7 10.2 %all-to-all-start = ((f32[128,1,512]{2,1,0:T(1,128)}), f32[128,1,512]{2,1,0:T(1,128)}, u32[]{:S(2)}, u32[]{:S(2)}) async-start(f32[128,1,512]{2,1,0:T(1,128)} %reshape.5162), calls=%async_computation | async-start | bytes 524288 | tf_op jit(solution)/shard_map/all_to_all | solution.py:20
  47.7 1.9 collective-permute-start
  49.6 7.0 %collective-permute-start.1 = (f32[11,768]{1,0:T(8,128)}, f32[11,768]{1,0:T(8,128)}, u32[]{:S(2)}, u32[]{:S(2)}) collective-permute-start(f32[11,768]{1,0:T(8,128)} %get-tuple-element.106), channel_id=1, source_target_pairs={{4,0},{8,4},{12,8},{16,12},{20,16},{24,20},{28,24},{32,28},{36,32}... | collective-permute-start | bytes 101384 | tf_op jit(solution)/shard_map/ppermute | solution.py:36
  75.7 1.6 multiply_divide_fusion.7
  78.8 2.0 multiply_divide_fusion.3
  81.0 2.7 divide_reduce_fusion.1
  83.7 2.3 multiply_divide_fusion.1
  87.8 5.4 %divide_reduce_fusion = f32[128,64]{1,0:T(8,128)S(1)} fusion(f32[128,64]{1,0:T(8,128)S(1)} %bitcast.632, f32[128,64]{1,0:T(8,128)S(1)} %copy-done.9, f32[128,64]{1,0:T(8,128)S(1)} %bitcast.635, f32[128,64]{1,0:T(8,128)S(1)} %copy-done.11, f32[128,64]{1,0:T(8,128)S(1)} %bitcast.629, f32[128,64]{1,0:T(8,128)S(1)} %copy-done.7), kind=kLoop, calls=%fused_computation.49 | loop fusion | flops 6283264 | bytes 229376 | tf_op jit(solution)/shard_map/reduce_sum | solution.py:50
  93.3 6.4 %multiply_divide_fusion = f32[128,64,64]{2,1,0:T(8,128)} fusion(f32[128,64]{1,0:T(8,128)S(1)} %divide_reduce_fusion, f32[128,64]{1,0:T(8,128)S(1)} %bitcast.633, f32[128,64]{1,0:T(8,128)S(1)} %copy-done.9, f32[128,64]{1,0:T(8,128)S(1)} %bitcast.636, f32[128,64]{1,0:T(8,128)S(1)} %copy-done.11, f32[128,64]{1,0:T(8,128)S(1)} %bitcast.630, ...), kind=kLoop, calls=%fused_computation.47 | loop fusion | flops 6291456 | bytes 2326528 | tf_op jit(solution)/shard_map/div | solution.py:50
  109.4 241.7 %while.10 = (s32[]{:T(128)}, f32[32,8,256]{2,1,0:T(8,128)}, s32[32,6]{1,0:T(8,128)}, f32[11,38,256]{2,0,1:T(8,128)S(1)}, f32[32,6]{1,0:T(8,128)}, /*index=5*/f32...) while((s32[]{:T(128)}, f32[32,8,256]{2,1,0:T(8,128)}, s32[32,6]{1,0:T(8,128)}, ...), condition=%wide.region_1.2_spmd, body=%wide.region_0.1_spmd.sunk | while | flops 42104376 | bytes 440149 | solution.py:76
  112.0 1.4 constant_dynamic-slice_fusion.91
  114.1 2.8 fusion.866
  119.6 1.4 constant_dynamic-slice_fusion.91
  121.6 2.8 fusion.866
  129.2 2.8 fusion.866
  136.7 2.8 fusion.866
  142.2 1.4 constant_dynamic-slice_fusion.91
  144.3 2.8 fusion.866
  149.7 1.4 constant_dynamic-slice_fusion.91
  151.8 2.8 fusion.866
  157.3 1.4 constant_dynamic-slice_fusion.91
  159.4 2.8 fusion.866
  166.9 2.8 fusion.866
  174.5 2.8 fusion.866
  179.9 1.4 constant_dynamic-slice_fusion.91
  182.0 2.8 fusion.866
  189.6 2.8 fusion.866
  197.1 2.8 fusion.866
  204.6 2.8 fusion.866
  212.2 2.8 fusion.866
  219.7 2.9 fusion.866
  227.3 2.8 fusion.866
  234.8 2.8 fusion.866
  242.4 2.8 fusion.866
  249.9 2.8 fusion.866
  257.5 2.8 fusion.866
  265.1 2.8 fusion.866
  272.6 2.8 fusion.866
  280.2 2.8 fusion.866
  287.8 2.8 fusion.866
  295.3 2.8 fusion.866
  302.9 2.8 fusion.866
  310.4 2.8 fusion.866
  318.0 2.8 fusion.866
  325.5 2.8 fusion.866
  333.1 2.8 fusion.866
  340.7 2.9 fusion.866
  348.2 2.8 fusion.866
  388.3 1.4 gather_fusion.13
  399.4 2.3 fusion.54
  401.8 2.6 convolution_add_fusion.1
  405.0 1.6 convolution_add_fusion.4
  406.6 2.6 convolution_add_fusion
  409.8 2.3 reduce.27
  412.3 11.2 %bitcast_reduce_fusion = f32[8,64,64]{2,0,1:T(8,128)S(1)} fusion(f32[128,64]{1,0:T(8,128)} %copy-done.27, f32[128,64]{1,0:T(8,128)S(1)} %bitcast.634, f32[128,64]{1,0:T(8,128)S(1)} %copy-done.10, f32[128,64]{1,0:T(8,128)S(1)} %bitcast.637, f32[128,64]{1,0:T(8,128)S(1)} %copy-done.12, f32[128,64]{1,0:T(8,128)S(1)} %bitcast.631, ...), kind=kOutput, calls=%fused_computation.131 | convolution fusion | flops 56655872 | bytes 622592 | tf_op jit(solution)/shard_map/qnr,nrs->qns/dot_general | solution.py:162
  423.6 5.1 %bitcast_reduce_fusion.1 = f32[8,32,64]{2,0,1:T(8,128)S(1)} fusion(f32[8,64,64]{2,0,1:T(8,128)S(1)} %bitcast_reduce_fusion, f32[64,64]{1,0:T(8,128)S(1)} %copy-done.55, f32[64,64]{1,0:T(8,128)S(1)} %bitcast.647, f32[64,64]{1,0:T(8,128)S(1)} %copy-done.16, f32[64,64]{1,0:T(8,128)S(1)} %bitcast.650, f32[64,64]{1,0:T(8,128)S(1)} %copy-done.18, ...), kind=kOutput, calls=%fused_computation.189 | convolution fusion | flops 28327936 | bytes 311296 | tf_op jit(solution)/shard_map/qnr,nrs->qns/dot_general | solution.py:162
  428.8 2.6 bitcast_reduce_fusion.2
  455.6 1.6 fusion.145
  458.7 3.2 fusion.17
  462.0 2.7 fusion.16
  (1060 shorter events, 259.8 us)
Async XLA Ops:
  0.9 33.5 %copy-start.158 = (f32[2,64]{1,0:T(2,128)}, f32[2,64]{1,0:T(2,128)S(1)}, u32[]{:S(2)}) copy-start(f32[2,64]{1,0:T(2,128)S(1)} %get-tuple-element.191) | copy-start | bytes 1540
  0.9 33.5 %copy-start.161 = (f32[2,64]{1,0:T(2,128)}, f32[2,64]{1,0:T(2,128)S(1)}, u32[]{:S(2)}) copy-start(f32[2,64]{1,0:T(2,128)S(1)} %get-tuple-element.192) | copy-start | bytes 1540
  0.9 33.5 %copy-start.164 = (f32[2,64]{1,0:T(2,128)}, f32[2,64]{1,0:T(2,128)S(1)}, u32[]{:S(2)}) copy-start(f32[2,64]{1,0:T(2,128)S(1)} %get-tuple-element.193) | copy-start | bytes 1540
  0.9 16.3 %copy-start.139 = (f32[4,64]{1,0:T(4,128)}, f32[4,64]{1,0:T(4,128)S(1)}, u32[]{:S(2)}) copy-start(f32[4,64]{1,0:T(4,128)S(1)} %get-tuple-element.194) | copy-start | bytes 3076
  0.9 16.3 %copy-start.142 = (f32[4,64]{1,0:T(4,128)}, f32[4,64]{1,0:T(4,128)S(1)}, u32[]{:S(2)}) copy-start(f32[4,64]{1,0:T(4,128)S(1)} %get-tuple-element.195) | copy-start | bytes 3076
  0.9 16.3 %copy-start.145 = (f32[4,64]{1,0:T(4,128)}, f32[4,64]{1,0:T(4,128)S(1)}, u32[]{:S(2)}) copy-start(f32[4,64]{1,0:T(4,128)S(1)} %get-tuple-element.196) | copy-start | bytes 3076
  0.9 15.2 %copy-start.115 = (f32[8,64]{1,0:T(8,128)}, f32[8,64]{1,0:T(8,128)S(1)}, u32[]{:S(2)}) copy-start(f32[8,64]{1,0:T(8,128)S(1)} %get-tuple-element.197) | copy-start | bytes 6148
  0.9 15.2 %copy-start.118 = (f32[8,64]{1,0:T(8,128)}, f32[8,64]{1,0:T(8,128)S(1)}, u32[]{:S(2)}) copy-start(f32[8,64]{1,0:T(8,128)S(1)} %get-tuple-element.198) | copy-start | bytes 6148
  1.0 15.2 %copy-start.121 = (f32[8,64]{1,0:T(8,128)}, f32[8,64]{1,0:T(8,128)S(1)}, u32[]{:S(2)}) copy-start(f32[8,64]{1,0:T(8,128)S(1)} %get-tuple-element.199) | copy-start | bytes 6148
  15.7 17.6 %copy-start.32 = (f32[3,16128]{1,0:T(4,128)S(1)}, f32[3,16128]{1,0:T(4,128)}, u32[]{:S(2)}) copy-start(f32[3,16128]{1,0:T(4,128)} %param.24) | copy-start | bytes 580612
  15.7 17.4 %copy-start.152 = (f32[4,2,64]{2,1,0:T(2,128)}, f32[4,2,64]{2,1,0:T(2,128)S(1)}, u32[]{:S(2)}) copy-start(f32[4,2,64]{2,1,0:T(2,128)S(1)} %broadcast_in_dim.228) | copy-start | bytes 6148
  15.7 17.4 %copy-start.154 = (f32[4,2,64]{2,1,0:T(2,128)}, f32[4,2,64]{2,1,0:T(2,128)S(1)}, u32[]{:S(2)}) copy-start(f32[4,2,64]{2,1,0:T(2,128)S(1)} %broadcast_in_dim.232) | copy-start | bytes 6148
  15.7 17.4 %copy-start.156 = (f32[4,2,64]{2,1,0:T(2,128)}, f32[4,2,64]{2,1,0:T(2,128)S(1)}, u32[]{:S(2)}) copy-start(f32[4,2,64]{2,1,0:T(2,128)S(1)} %broadcast_in_dim.230) | copy-start | bytes 6148
  16.9 16.3 %copy-start.169 = (f32[2,2,64]{2,1,0:T(2,128)}, f32[2,2,64]{2,1,0:T(2,128)S(1)}, u32[]{:S(2)}) copy-start(f32[2,2,64]{2,1,0:T(2,128)S(1)} %broadcast_in_dim.234) | copy-start | bytes 3076
  16.9 16.3 %copy-start.171 = (f32[2,2,64]{2,1,0:T(2,128)}, f32[2,2,64]{2,1,0:T(2,128)S(1)}, u32[]{:S(2)}) copy-start(f32[2,2,64]{2,1,0:T(2,128)S(1)} %broadcast_in_dim.238) | copy-start | bytes 3076
  16.9 16.3 %copy-start.173 = (f32[2,2,64]{2,1,0:T(2,128)}, f32[2,2,64]{2,1,0:T(2,128)S(1)}, u32[]{:S(2)}) copy-start(f32[2,2,64]{2,1,0:T(2,128)S(1)} %broadcast_in_dim.236) | copy-start | bytes 3076
  17.2 16.0 %copy-start.197 = (f32[4,64]{1,0:T(4,128)}, f32[4,64]{1,0:T(4,128)S(1)}, u32[]{:S(2)}) copy-start(f32[4,64]{1,0:T(4,128)S(1)} %divide_reduce_fusion.9) | copy-start | bytes 3076
  17.7 29.3 %copy-start.2 = (f32[8,8192]{1,0:T(8,128)S(1)}, f32[8,8192]{1,0:T(8,128)}, u32[]{:S(2)}) copy-start(f32[8,8192]{1,0:T(8,128)} %param.19) | copy-start | bytes 786436
  17.7 29.3 %copy-start.20 = (f32[3,8192]{1,0:T(4,128)S(1)}, f32[3,8192]{1,0:T(4,128)}, u32[]{:S(2)}) copy-start(f32[3,8192]{1,0:T(4,128)} %param.20) | copy-start | bytes 294916
  17.7 333.3 %collective-permute-start.3 = (f32[11,62,64]{2,0,1:T(8,128)S(1)}, f32[11,62,64]{2,0,1:T(8,128)}, u32[]{:S(2)}, u32[]{:S(2)}) collective-permute-start(f32[11,62,64]{2,0,1:T(8,128)S(1)} %maximum_maximum_fusion), channel_id=1, source_target_pairs={{4,0},{8,4},{12,8},{16,12},{20,16},{24,20},{28,24},{32,28},{36,32}... | collective-permute-start | bytes 523784 | tf_op jit(solution)/shard_map/ppermute | solution.py:36
  31.2 320.7 %collective-permute-start.2 = (f32[11,62,64]{2,0,1:T(8,128)S(1)}, f32[11,62,64]{2,0,1:T(8,128)}, u32[]{:S(2)}, u32[]{:S(2)}) collective-permute-start(f32[11,62,64]{2,0,1:T(8,128)S(1)} %maximum_maximum_fusion), channel_id=1, source_target_pairs={{0,4},{4,8},{8,12},{12,16},{16,20},{20,24},{24,28},{28,32},{32,36}... | collective-permute-start | bytes 523784 | tf_op jit(solution)/shard_map/ppermute | solution.py:35
  33.5 32.1 %copy-start = (f32[3,252,64]{2,1,0:T(8,128)}, f32[3,252,64]{2,1,0:T(8,128)S(1)}, u32[]{:S(2)}) copy-start(f32[3,252,64]{2,1,0:T(8,128)S(1)} %reshape.4905) | copy-start | bytes 580612
  33.5 29.4 %copy-start.184 = (s32[32,3]{0,1:T(4,128)S(1)}, s32[32,3]{0,1:T(4,128)}, u32[]{:S(2)}) copy-start(s32[32,3]{0,1:T(4,128)} %param.25) | copy-start | bytes 1156
  33.5 30.7 %copy-start.185 = (s32[32,6]{0,1:T(8,128)S(1)}, s32[32,6]{0,1:T(8,128)}, u32[]{:S(2)}) copy-start(s32[32,6]{0,1:T(8,128)} %param.21) | copy-start | bytes 2308
  36.7 372.5 %all-to-all-start = ((f32[128,1,512]{2,1,0:T(1,128)}), f32[128,1,512]{2,1,0:T(1,128)}, u32[]{:S(2)}, u32[]{:S(2)}) async-start(f32[128,1,512]{2,1,0:T(1,128)} %reshape.5162), calls=%async_computation | async-start | bytes 524288 | tf_op jit(solution)/shard_map/all_to_all | solution.py:20
  47.0 33.8 %copy-start.1 = (f32[11,8192]{1,0:T(8,128)}, f32[11,8192]{1,0:T(8,128)S(1)}, u32[]{:S(2)}) copy-start(f32[11,8192]{1,0:T(8,128)S(1)} %constant_dynamic-update-slice_fusion) | copy-start | bytes 1081348
  47.7 58.5 %collective-permute-start = (f32[11,768]{1,0:T(8,128)}, f32[11,768]{1,0:T(8,128)}, u32[]{:S(2)}, u32[]{:S(2)}) collective-permute-start(f32[11,768]{1,0:T(8,128)} %get-tuple-element.105), channel_id=1, source_target_pairs={{0,4},{4,8},{8,12},{12,16},{16,20},{20,24},{24,28},{28,32},{32,36}... | collective-permute-start | bytes 101384 | tf_op jit(solution)/shard_map/ppermute | solution.py:35
  49.6 56.6 %collective-permute-start.1 = (f32[11,768]{1,0:T(8,128)}, f32[11,768]{1,0:T(8,128)}, u32[]{:S(2)}, u32[]{:S(2)}) collective-permute-start(f32[11,768]{1,0:T(8,128)} %get-tuple-element.106), channel_id=1, source_target_pairs={{4,0},{8,4},{12,8},{16,12},{20,16},{24,20},{28,24},{32,28},{36,32}... | collective-permute-start | bytes 101384 | tf_op jit(solution)/shard_map/ppermute | solution.py:36
  65.5 15.5 %copy-start.60 = (f32[16,64]{1,0:T(8,128)}, f32[16,64]{1,0:T(8,128)S(1)}, u32[]{:S(2)}) copy-start(f32[16,64]{1,0:T(8,128)S(1)} %get-tuple-element.115) | copy-start | bytes 12292
  65.5 18.2 %copy-start.28 = (f32[32,64]{1,0:T(8,128)}, f32[32,64]{1,0:T(8,128)S(1)}, u32[]{:S(2)}) copy-start(f32[32,64]{1,0:T(8,128)S(1)} %get-tuple-element.117) | copy-start | bytes 24580
  65.5 20.5 %copy-start.30 = (f32[32,64]{1,0:T(8,128)}, f32[32,64]{1,0:T(8,128)S(1)}, u32[]{:S(2)}) copy-start(f32[32,64]{1,0:T(8,128)S(1)} %get-tuple-element.118) | copy-start | bytes 24580
  65.6 18.1 %copy-start.15 = (f32[64,64]{1,0:T(8,128)}, f32[64,64]{1,0:T(8,128)S(1)}, u32[]{:S(2)}) copy-start(f32[64,64]{1,0:T(8,128)S(1)} %get-tuple-element.123) | copy-start | bytes 49156
  65.6 18.1 %copy-start.17 = (f32[64,64]{1,0:T(8,128)}, f32[64,64]{1,0:T(8,128)S(1)}, u32[]{:S(2)}) copy-start(f32[64,64]{1,0:T(8,128)S(1)} %get-tuple-element.124) | copy-start | bytes 49156
  65.6 20.5 %copy-start.13 = (f32[64,64]{1,0:T(8,128)}, f32[64,64]{1,0:T(8,128)S(1)}, u32[]{:S(2)}) copy-start(f32[64,64]{1,0:T(8,128)S(1)} %get-tuple-element.122) | copy-start | bytes 49156
  351.1 22.9 %copy-start.224 = (pred[8]{0:T(512)(128)(4,1)S(1)}, pred[8]{0:T(512)(128)(4,1)}, u32[]{:S(2)}) copy-start(pred[8]{0:T(512)(128)(4,1)} %get-tuple-element.271) | copy-start | bytes 28
  351.1 23.6 %copy-start.223 = (pred[8]{0:T(512)(128)(4,1)S(1)}, pred[8]{0:T(512)(128)(4,1)}, u32[]{:S(2)}) copy-start(pred[8]{0:T(512)(128)(4,1)} %compare_and_fusion.9) | copy-start | bytes 28
  351.1 26.8 %copy-start.19 = (f32[11,16,64]{2,0,1:T(8,128)S(1)}, f32[11,16,64]{2,0,1:T(8,128)}, u32[]{:S(2)}) copy-start(f32[11,16,64]{2,0,1:T(8,128)} %slice.1348) | copy-start | bytes 135172
  433.6 17.1 %copy-start.160 = (f32[2,64]{1,0:T(2,128)S(1)}, f32[2,64]{1,0:T(2,128)}, u32[]{:S(2)}) copy-start(f32[2,64]{1,0:T(2,128)} %copy-done.158) | copy-start | bytes 1540
  433.6 17.1 %copy-start.163 = (f32[2,64]{1,0:T(2,128)S(1)}, f32[2,64]{1,0:T(2,128)}, u32[]{:S(2)}) copy-start(f32[2,64]{1,0:T(2,128)} %copy-done.161) | copy-start | bytes 1540
  433.6 17.1 %copy-start.166 = (f32[2,64]{1,0:T(2,128)S(1)}, f32[2,64]{1,0:T(2,128)}, u32[]{:S(2)}) copy-start(f32[2,64]{1,0:T(2,128)} %copy-done.164) | copy-start | bytes 1540
  433.6 17.1 %copy-start.209 = (f32[64]{0:T(128)S(1)}, f32[64]{0:T(128)}, u32[]{:S(2)}) copy-start(f32[64]{0:T(128)} %copy-done.208) | copy-start | bytes 772
  433.6 17.1 %copy-start.211 = (f32[64]{0:T(128)S(1)}, f32[64]{0:T(128)}, u32[]{:S(2)}) copy-start(f32[64]{0:T(128)} %copy-done.210) | copy-start | bytes 772
  433.6 17.1 %copy-start.213 = (f32[64]{0:T(128)S(1)}, f32[64]{0:T(128)}, u32[]{:S(2)}) copy-start(f32[64]{0:T(128)} %copy-done.212) | copy-start | bytes 772
  433.7 17.1 %copy-start.216 = (f32[2,64]{1,0:T(2,128)S(1)}, f32[2,64]{1,0:T(2,128)}, u32[]{:S(2)}) copy-start(f32[2,64]{1,0:T(2,128)} %copy-done.215) | copy-start | bytes 1540
  433.7 15.5 %copy-start.241 = (f32[64]{0:T(128)S(1)}, f32[64]{0:T(128)}, u32[]{:S(2)}) copy-start(f32[64]{0:T(128)} %get-tuple-element.141) | copy-start | bytes 772
  433.7 16.7 %copy-start.239 = (f32[64]{0:T(128)S(1)}, f32[64]{0:T(128)}, u32[]{:S(2)}) copy-start(f32[64]{0:T(128)} %get-tuple-element.137) | copy-start | bytes 772
  433.7 16.7 %copy-start.240 = (f32[64]{0:T(128)S(1)}, f32[64]{0:T(128)}, u32[]{:S(2)}) copy-start(f32[64]{0:T(128)} %get-tuple-element.138) | copy-start | bytes 772
  434.9 14.3 %copy-start.242 = (f32[64]{0:T(128)S(1)}, f32[64]{0:T(128)}, u32[]{:S(2)}) copy-start(f32[64]{0:T(128)} %get-tuple-element.143) | copy-start | bytes 772
  434.9 14.3 %copy-start.244 = (f32[64]{0:T(128)S(1)}, f32[64]{0:T(128)}, u32[]{:S(2)}) copy-start(f32[64]{0:T(128)} %get-tuple-element.147) | copy-start | bytes 772
  434.9 15.2 %copy-start.245 = (f32[64]{0:T(128)S(1)}, f32[64]{0:T(128)}, u32[]{:S(2)}) copy-start(f32[64]{0:T(128)} %get-tuple-element.139) | copy-start | bytes 772
  435.0 15.2 %copy-start.246 = (f32[64]{0:T(128)S(1)}, f32[64]{0:T(128)}, u32[]{:S(2)}) copy-start(f32[64]{0:T(128)} %get-tuple-element.140) | copy-start | bytes 772
  435.0 15.2 %copy-start.247 = (f32[64]{0:T(128)S(1)}, f32[64]{0:T(128)}, u32[]{:S(2)}) copy-start(f32[64]{0:T(128)} %get-tuple-element.146) | copy-start | bytes 772
  435.0 15.5 %copy-start.243 = (f32[64]{0:T(128)S(1)}, f32[64]{0:T(128)}, u32[]{:S(2)}) copy-start(f32[64]{0:T(128)} %get-tuple-element.145) | copy-start | bytes 772
  435.0 16.2 %copy-start.135 = (f32[11,2,64]{2,0,1:T(8,128)S(1)}, f32[11,2,64]{2,0,1:T(8,128)}, u32[]{:S(2)}) copy-start(f32[11,2,64]{2,0,1:T(8,128)} %copy-done.134) | copy-start | bytes 16900
  435.0 16.2 %copy-start.217 = (f32[1,2,64]{2,0,1:T(1,128)S(1)}, f32[1,2,64]{2,0,1:T(1,128)}, u32[]{:S(2)}) copy-start(f32[1,2,64]{2,0,1:T(1,128)} %get-tuple-element.224) | copy-start | bytes 1540
  435.0 16.2 %copy-start.218 = (f32[1,2,64]{2,0,1:T(1,128)S(1)}, f32[1,2,64]{2,0,1:T(1,128)}, u32[]{:S(2)}) copy-start(f32[1,2,64]{2,0,1:T(1,128)} %get-tuple-element.225) | copy-start | bytes 1540
  435.0 16.2 %copy-start.219 = (f32[1,2,64]{2,0,1:T(1,128)S(1)}, f32[1,2,64]{2,0,1:T(1,128)}, u32[]{:S(2)}) copy-start(f32[1,2,64]{2,0,1:T(1,128)} %get-tuple-element.226) | copy-start | bytes 1540
  436.9 15.3 %copy-start.141 = (f32[4,64]{1,0:T(4,128)S(1)}, f32[4,64]{1,0:T(4,128)}, u32[]{:S(2)}) copy-start(f32[4,64]{1,0:T(4,128)} %copy-done.139) | copy-start | bytes 3076
  436.9 15.3 %copy-start.144 = (f32[4,64]{1,0:T(4,128)S(1)}, f32[4,64]{1,0:T(4,128)}, u32[]{:S(2)}) copy-start(f32[4,64]{1,0:T(4,128)} %copy-done.142) | copy-start | bytes 3076
  436.9 15.3 %copy-start.147 = (f32[4,64]{1,0:T(4,128)S(1)}, f32[4,64]{1,0:T(4,128)}, u32[]{:S(2)}) copy-start(f32[4,64]{1,0:T(4,128)} %copy-done.145) | copy-start | bytes 3076
  436.9 15.3 %copy-start.170 = (f32[2,2,64]{2,1,0:T(2,128)S(1)}, f32[2,2,64]{2,1,0:T(2,128)}, u32[]{:S(2)}) copy-start(f32[2,2,64]{2,1,0:T(2,128)} %copy-done.169) | copy-start | bytes 3076
  436.9 15.3 %copy-start.172 = (f32[2,2,64]{2,1,0:T(2,128)S(1)}, f32[2,2,64]{2,1,0:T(2,128)}, u32[]{:S(2)}) copy-start(f32[2,2,64]{2,1,0:T(2,128)} %copy-done.171) | copy-start | bytes 3076
  436.9 15.3 %copy-start.174 = (f32[2,2,64]{2,1,0:T(2,128)S(1)}, f32[2,2,64]{2,1,0:T(2,128)}, u32[]{:S(2)}) copy-start(f32[2,2,64]{2,1,0:T(2,128)} %copy-done.173) | copy-start | bytes 3076
  436.9 15.3 %copy-start.198 = (f32[4,64]{1,0:T(4,128)S(1)}, f32[4,64]{1,0:T(4,128)}, u32[]{:S(2)}) copy-start(f32[4,64]{1,0:T(4,128)} %copy-done.197) | copy-start | bytes 3076
  (199 other events, 931.1 us)
